TPU v7x, 32 devices: a whole 2x2x4 slice. The times are simulated.
32 devices in a mesh: tensor: 4 (over z), example: 8 (over y, x, core).
Axes of the slice: x: 2, y: 2, z: 4, core: 2. Of those that a mesh axis runs over, the one named last changes fastest.
Arguments:
- queries: bfloat16 [1, 4096, 4096], P(None, 'example', 'tensor'), may hold values from -0.0014648438 to 0.0014648438
- basis_out: bfloat16 [4096, 4096], P('example', 'tensor'), may hold values from -0.09375 to 0.09375
- basis_in: bfloat16 [4096, 4096], P('tensor', 'example'), may hold values from -0.09375 to 0.09375
- eigvals: float32 [4096, 4096], P('tensor', 'example'), may hold values from 0.25 to 4
- input_fac: bfloat16 [128, 8, 4096], P('example', None, 'tensor'), may hold values from -6 to 6
- grad_fac: bfloat16 [128, 8, 4096], P('example', None, 'tensor'), may hold values from -6 to 6
- cand_slot: int32 [128], replicated, may hold values from 0 to 127, as said below
- score_list: int32 [8, 16], replicated, may hold values from 0 to 127, as said below
- token_count: int32 [128], replicated, may hold values from 1 to 8
Outputs:
- scores: float32 [1, 128, 8], P(None, 'example')
Inputs may be any that keep to these rules, and one draw needn't show every extreme that they name: `cand_slot`: a permutation; slot s belongs to owner s // 16. `score_list`: every candidate appears exactly once; a scorer's list holds at most 4 candidates of any one owner, and some scorer takes exactly 4 from some owner.
All inputs are finite; a program needn't handle non-finite values.
Results may differ from a plain program's by a relative error of at most 0.019.
Values may be sent and summed in bfloat16 or wider, within the bound.
A program may use at most 128 MiB of HBM per device.

v0:
```python
import jax
import jax.numpy as jnp
from jax import lax
from jax.sharding import PartitionSpec as P


def body(
    queries, basis_out, basis_in, eigvals, input_fac, grad_fac, cand_slot, score_list, token_count
):
    ex_count = lax.axis_size("example")
    my_index = lax.axis_index("example")
    out_rows = lax.all_gather(basis_out, "tensor", axis=1, tiled=True)
    in_rows = lax.all_gather(basis_in, "example", axis=1, tiled=True)
    query_total = queries.shape[0]
    columns = out_rows
    rotated = lax.psum_scatter(
        jnp.einsum("ki,qkj->iqj", columns, queries, preferred_element_type=jnp.float32).astype(
            jnp.bfloat16
        ),
        "example",
        scatter_dimension=0,
        tiled=True,
    )
    columns = in_rows
    core_sum = lax.psum_scatter(
        jnp.einsum("kj,iqk->jqi", columns, rotated, preferred_element_type=jnp.float32).astype(
            jnp.bfloat16
        ),
        "tensor",
        scatter_dimension=0,
        tiled=True,
    ).astype(jnp.float32)
    scaled = (core_sum / eigvals[:, None, :]).astype(jnp.bfloat16)
    columns = out_rows
    turned = jnp.einsum(
        "jqk,ik->jqi",
        lax.all_gather(scaled, "example", axis=2, tiled=True),
        columns,
        preferred_element_type=jnp.float32,
    ).astype(jnp.bfloat16)
    columns = in_rows
    precond = jnp.einsum(
        "jk,kqi->jqi",
        columns,
        lax.all_gather(turned, "tensor", axis=0, tiled=True),
        preferred_element_type=jnp.float32,
    ).astype(jnp.bfloat16)
    cand_total = cand_slot.shape[0]
    cand_dev = input_fac.shape[0]
    token_len = input_fac.shape[1]
    shard_width = input_fac.shape[2]
    list_len = score_list.shape[1]
    cand_ids = jnp.arange(cand_total, dtype=jnp.int32)
    matches = (score_list[:, :, None] == cand_ids[None, None, :]).astype(jnp.int32)
    entry_slot = jnp.sum(matches * cand_slot[None, None, :], axis=2)
    entry_count = jnp.sum(matches * token_count[None, None, :], axis=2)
    entry_owner = entry_slot // cand_dev
    entry_local = entry_slot % cand_dev
    earlier = jnp.arange(list_len)[:, None] > jnp.arange(list_len)[None, :]
    same_owner = entry_owner[:, :, None] == entry_owner[:, None, :]
    entry_rank = jnp.sum((same_owner & earlier[None]).astype(jnp.int32), axis=2)
    capacity = 2 * cand_dev // ex_count
    place_ids = jnp.arange(capacity, dtype=jnp.int32)
    local_ids = jnp.arange(cand_dev, dtype=jnp.int32)
    owned_here = entry_owner == my_index
    send_table = jnp.sum(
        (
            owned_here[:, :, None, None]
            & (entry_rank[:, :, None, None] == place_ids[None, None, :, None])
            & (entry_local[:, :, None, None] == local_ids[None, None, None, :])
        ).astype(jnp.float32),
        axis=1,
    )
    my_owner = lax.dynamic_index_in_dim(entry_owner, my_index, 0, keepdims=False)
    my_rank = lax.dynamic_index_in_dim(entry_rank, my_index, 0, keepdims=False)
    my_count = lax.dynamic_index_in_dim(entry_count, my_index, 0, keepdims=False)
    source_ids = jnp.arange(ex_count, dtype=jnp.int32)
    take_table = (
        (
            (my_owner[:, None, None] == source_ids[None, :, None])
            & (my_rank[:, None, None] == place_ids[None, None, :])
        )
        .astype(jnp.float32)
        .reshape(list_len, ex_count * capacity)
    )
    select_send = send_table.astype(jnp.bfloat16)
    select_take = take_table.astype(jnp.bfloat16)

    def route_rows(owned_rows):
        return jnp.einsum(
            "ers,sx->erx", select_send, owned_rows, preferred_element_type=jnp.float32
        ).astype(jnp.bfloat16)

    def collect_rows(received):
        flat_received = received.reshape(ex_count * capacity, received.shape[2])
        return jnp.dot(select_take, flat_received, preferred_element_type=jnp.float32).astype(
            jnp.bfloat16
        )

    flat_acts = input_fac.reshape(cand_dev, token_len * shard_width)
    flat_grads = grad_fac.reshape(cand_dev, token_len * shard_width)
    sent_acts, sent_grads = (
        lax.all_to_all(route_rows(flat_acts), "example", split_axis=0, concat_axis=0, tiled=True),
        lax.all_to_all(route_rows(flat_grads), "example", split_axis=0, concat_axis=0, tiled=True),
    )
    got_acts = collect_rows(sent_acts).reshape(list_len * token_len, shard_width)
    got_grads = collect_rows(sent_grads).reshape(list_len * token_len, shard_width)
    whole_grads = lax.all_gather(got_grads, "tensor", axis=1, tiled=True)
    columns = whole_grads
    weighted = jnp.einsum(
        "tn,jqn->qtj",
        columns,
        lax.all_gather(precond, "example", axis=2, tiled=True),
        preferred_element_type=jnp.float32,
    )
    partial_scores = jnp.sum(got_acts.astype(jnp.float32)[None] * weighted, axis=2)
    summed = lax.psum(partial_scores, "tensor").reshape(query_total, list_len, token_len)
    live_mask = jnp.arange(token_len, dtype=jnp.int32)[None, :] < my_count[:, None]
    return jnp.where(live_mask[None], summed, jnp.float32(0.0))


def solution(mesh):
    in_specs = (
        P(None, "example", "tensor"),
        P("example", "tensor"),
        P("tensor", "example"),
        P("tensor", "example"),
        P("example", None, "tensor"),
        P("example", None, "tensor"),
        P(),
        P(),
        P(),
    )
    out_specs = P(None, "example", None)
    return jax.shard_map(body, mesh=mesh, in_specs=in_specs, out_specs=out_specs, check_vma=False)
```

profile of v0, /device:TPU:0, one launch (start us, length us, event | category | flops | bytes accessed | tf_op | source)
XLA Modules:
  0.0 568.8 jit_solution(2000959011714621672)
XLA Ops:
  6.5 0.0 copy-start
  6.5 0.0 all-gather.9.cloned.1.call-start
  6.5 0.7 all-gather.9.cloned.1.call-update
  7.3 0.0 all-gather.11.cloned.1.call-start
  7.3 0.7 all-gather.11.cloned.1.call-update
  8.0 0.0 reduce-scatter.3.cloned.1.call-start
  8.1 84.4 %all-gather.9.cloned.1.call-done = bf16[512,4096]{1,0:T(8,128)(2,1)} async-done(((bf16[512,1024]{1,0:T(8,128)(2,1)}), bf16[512,4096]{1,0:T(8,128)(2,1)}) %all-gather.9.cloned.1.call-update) | async-done | bytes 4194320 | tf_op jit(solution)/shard_map/all_gather | solution.py:12
  92.4 0.0 copy-done
  92.4 9.0 %convert_bitcast_fusion = bf16[4096,1,1024]{2,0,1:T(8,128)(2,1)} fusion(bf16[512,4096]{1,0:T(8,128)(2,1)} %all-gather.9.cloned.1.call-done, bf16[1,512,1024]{2,1,0:T(8,128)(2,1)S(1)} %copy-done), kind=kOutput, calls=%fused_computation.9 | convolution fusion | flops 4299161600 | bytes 13631488 | tf_op jit(solution)/shard_map/ki,qkj->iqj/dot_general | solution.py:17
  101.4 0.0 reduce-scatter.3.cloned.1.call-update
  101.4 0.0 reduce-scatter.5.cloned.1.call-start
  101.5 47.3 %all-gather.11.cloned.1.call-done = bf16[1024,4096]{1,0:T(8,128)(2,1)} async-done(((bf16[1024,512]{1,0:T(8,128)(2,1)}), bf16[1024,4096]{1,0:T(8,128)(2,1)}) %all-gather.11.cloned.1.call-update) | async-done | bytes 8388624 | tf_op jit(solution)/shard_map/all_gather | solution.py:13
  148.8 74.8 %reduce-scatter.3.cloned.1.call-done = bf16[512,1,1024]{2,0,1:T(8,128)(2,1)} async-done(((bf16[4096,1,1024]{2,0,1:T(8,128)(2,1)}), bf16[512,1,1024]{2,0,1:T(8,128)(2,1)}) %reduce-scatter.3.cloned.1.call-update) | async-done | bytes 1048592 | tf_op jit(solution)/shard_map/reduce_scatter | solution.py:16
  223.6 10.2 %fusion.5 = bf16[4096,1,512]{0,2,1:T(8,128)(2,1)} fusion(bf16[1024,4096]{1,0:T(8,128)(2,1)} %all-gather.11.cloned.1.call-done, bf16[512,1,1024]{2,0,1:T(8,128)(2,1)} %reduce-scatter.3.cloned.1.call-done), kind=kOutput, calls=%fused_computation.11 | convolution fusion | flops 4297064448 | bytes 13631488 | tf_op jit(solution)/shard_map/kj,iqk->jqi/dot_general | solution.py:26
  233.8 0.0 reduce-scatter.5.cloned.1.call-update
  233.8 0.0 all-gather.13.cloned.1.call-start
  233.9 1.9 copy.26
  235.8 74.9 %reduce-scatter.5.cloned.1.call-done = bf16[1024,1,512]{0,2,1:T(8,128)(2,1)} async-done(((bf16[4096,1,512]{0,2,1:T(8,128)(2,1)}), bf16[1024,1,512]{0,2,1:T(8,128)(2,1)}) %reduce-scatter.5.cloned.1.call-update) | async-done | bytes 1048592 | tf_op jit(solution)/shard_map/reduce_scatter | solution.py:25
  310.7 2.6 fusion.6
  313.3 0.0 all-gather.13.cloned.1.call-update
  313.4 0.0 copy-start.1
  313.4 0.0 copy-start.3
  313.4 0.0 copy-start.4
  313.4 0.0 copy-start.5
  313.4 0.2 all-gather.17.cloned.1.call-start
  313.6 54.8 %all-gather.13.cloned.1.call-done = bf16[1024,1,4096]{0,2,1:T(8,128)(2,1)} async-done(((bf16[1024,1,512]{0,2,1:T(8,128)(2,1)}), bf16[1024,1,4096]{0,2,1:T(8,128)(2,1)}) %all-gather.13.cloned.1.call-update) | async-done | bytes 8388624 | tf_op jit(solution)/shard_map/all_gather | solution.py:37
  368.4 10.1 %fusion.7 = bf16[1024,512]{1,0:T(8,128)(2,1)} fusion(bf16[512,4096]{1,0:T(8,128)(2,1)} %all-gather.9.cloned.1.call-done, bf16[1024,1,4096]{0,2,1:T(8,128)(2,1)} %all-gather.13.cloned.1.call-done), kind=kOutput, calls=%fused_computation.14 | convolution fusion | flops 4295491584 | bytes 13631488 | tf_op jit(solution)/shard_map/jqk,ik->jqi/dot_general | solution.py:35
  378.5 0.0 all-gather.17.cloned.1.call-update
  378.5 0.0 copy-done.1
  378.5 0.1 reshape.275
  378.7 0.0 copy-done.3
  378.7 0.0 copy-done.4
  378.7 0.4 select_reduce_fusion.1
  379.1 0.3 convert_reduce_fusion.1
  379.5 0.1 iota_compare_fusion
  379.5 0.2 convert_reduce_fusion
  379.7 0.3 convolution_convert_fusion
  380.0 1.2 copy.28
  381.2 3.5 all-to-all-start.1
  384.7 0.0 all-gather.15.cloned.1.call-start
  384.8 9.6 %all-to-all-done.1 = bf16[8,4,8192]{2,1,0:T(4,128)(2,1)S(1)} async-done(((bf16[8,4,8192]{2,1,0:T(4,128)(2,1)}), bf16[8,4,8192]{2,1,0:T(4,128)(2,1)S(1)}, u32[]{:S(2)}, u32[]{:S(2)}) %all-to-all-start.1) | async-done | bytes 524320 | tf_op jit(solution)/shard_map/all_to_all | solution.py:104
  394.4 0.4 fusion.2
  394.8 0.9 reshape.265
  395.6 0.0 all-gather.15.cloned.1.call-update
  395.7 0.0 copy-start.2
  395.7 0.3 all-gather.19.cloned.1.call-start
  396.0 63.5 %all-gather.17.cloned.1.call-done = bf16[4096,512]{1,0:T(8,128)(2,1)} async-done(((bf16[1024,512]{1,0:T(8,128)(2,1)}), bf16[4096,512]{1,0:T(8,128)(2,1)}) %all-gather.17.cloned.1.call-update) | async-done | bytes 4194320 | tf_op jit(solution)/shard_map/all_gather | solution.py:45
  459.4 10.2 %fusion.10 = bf16[1024,512]{0,1:T(8,128)(2,1)} fusion(bf16[4096,512]{1,0:T(8,128)(2,1)} %all-gather.17.cloned.1.call-done, bf16[1024,4096]{1,0:T(8,128)(2,1)} %all-gather.11.cloned.1.call-done), kind=kOutput, calls=%fused_computation.16 | convolution fusion | flops 4295491584 | bytes 13631488 | tf_op jit(solution)/shard_map/jk,kqi->jqi/dot_general | solution.py:42
  469.6 0.0 all-gather.19.cloned.1.call-update
  469.6 0.1 reshape.273
  469.8 0.3 convolution_convert_fusion.1
  470.1 1.2 copy.24
  471.3 3.7 all-to-all-start
  475.0 9.7 %all-to-all-done = bf16[8,4,8192]{2,1,0:T(4,128)(2,1)S(1)} async-done(((bf16[8,4,8192]{2,1,0:T(4,128)(2,1)}), bf16[8,4,8192]{2,1,0:T(4,128)(2,1)S(1)}, u32[]{:S(2)}, u32[]{:S(2)}) %all-to-all-start) | async-done | bytes 524320 | tf_op jit(solution)/shard_map/all_to_all | solution.py:103
  484.7 0.4 fusion.1
  485.1 0.1 reshape.268
  485.3 0.2 copy.30
  485.4 2.0 all-gather.15.cloned.1.call-done
  487.5 55.8 %all-gather.19.cloned.1.call-done = bf16[1024,4096]{0,1:T(8,128)(2,1)} async-done(((bf16[1024,512]{0,1:T(8,128)(2,1)}), bf16[1024,4096]{0,1:T(8,128)(2,1)}) %all-gather.19.cloned.1.call-update) | async-done | bytes 8388624 | tf_op jit(solution)/shard_map/all_gather | solution.py:113
  543.3 6.0 %fusion.12 = f32[128]{0:T(128)S(1)} fusion(f32[1,128,1024]{1,2,0:T(8,128)S(1)} %copy.30, bf16[1024,4096]{0,1:T(8,128)(2,1)} %all-gather.19.cloned.1.call-done, bf16[128,4096]{1,0:T(8,128)(2,1)} %all-gather.15.cloned.1.call-done), kind=kOutput, calls=%fused_computation.19 | convolution fusion | flops 1074003840 | bytes 9961984 | tf_op jit(solution)/shard_map/tn,jqn->qtj/dot_general | solution.py:110
  549.3 0.1 reshape.266
  549.4 11.8 %psum.7 = f32[1,16,8]{2,1,0:T(8,128)S(1)} all-reduce(f32[1,16,8]{2,1,0:T(8,128)S(1)} %reshape.266), channel_id=1, replica_groups=mesh['tensor'=4,'example'=8] {'tensor'}, use_global_device_ids=true, to_apply=%region_7.8 | all-reduce | flops 128 | bytes 1024 | tf_op jit(solution)/shard_map/psum | solution.py:117
  561.2 0.1 fusion.18
  561.3 0.7 copy.31
  (10 shorter events, 0.1 us)
Async XLA Ops:
  6.5 85.9 %copy-start = (bf16[1,512,1024]{2,1,0:T(8,128)(2,1)S(1)}, bf16[1,512,1024]{2,1,0:T(8,128)(2,1)}, u32[]{:S(2)}) copy-start(bf16[1,512,1024]{2,1,0:T(8,128)(2,1)} %param.9) | copy-start | bytes 3145732
  6.5 85.9 %all-gather.9.cloned.1.call-start = ((), (), s32[]{:S(2)}) async-start(), calls=%async_computation.4 | async-start | bytes 5242880 | tf_op jit(solution)/shard_map/all_gather | solution.py:12
  7.3 141.6 %all-gather.11.cloned.1.call-start = ((), (), s32[]{:S(2)}) async-start(), calls=%async_computation.6 | async-start | bytes 9437184 | tf_op jit(solution)/shard_map/all_gather | solution.py:13
  8.0 215.6 %reduce-scatter.3.cloned.1.call-start = ((), (), s32[]{:S(2)}) async-start(), calls=%async_computation.5 | async-start | bytes 9437184 | tf_op jit(solution)/shard_map/reduce_scatter | solution.py:16
  101.4 209.3 %reduce-scatter.5.cloned.1.call-start = ((), (), s32[]{:S(2)}) async-start(), calls=%async_computation.7 | async-start | bytes 5242880 | tf_op jit(solution)/shard_map/reduce_scatter | solution.py:25
  233.8 134.6 %all-gather.13.cloned.1.call-start = ((), (), s32[]{:S(2)}) async-start(), calls=%async_computation.8 | async-start | bytes 9437184 | tf_op jit(solution)/shard_map/all_gather | solution.py:37
  313.4 65.1 %copy-start.1 = (bf16[16,8,1024]{2,1,0:T(8,128)(2,1)S(1)}, bf16[16,8,1024]{2,1,0:T(8,128)(2,1)}, u32[]{:S(2)}) copy-start(bf16[16,8,1024]{2,1,0:T(8,128)(2,1)} %param.14) | copy-start | bytes 786436
  313.4 65.3 %copy-start.3 = (s32[8,16]{1,0:T(8,128)S(1)}, s32[8,16]{1,0:T(8,128)}, u32[]{:S(2)}) copy-start(s32[8,16]{1,0:T(8,128)} %param.16) | copy-start | bytes 1540
  313.4 65.3 %copy-start.4 = (s32[128]{0:T(128)S(1)}, s32[128]{0:T(128)}, u32[]{:S(2)}) copy-start(s32[128]{0:T(128)} %param.17) | copy-start | bytes 1540
  313.4 65.3 %copy-start.5 = (s32[128]{0:T(128)S(1)}, s32[128]{0:T(128)}, u32[]{:S(2)}) copy-start(s32[128]{0:T(128)} %param.15) | copy-start | bytes 1540
  313.4 146.0 %all-gather.17.cloned.1.call-start = ((), (), s32[]{:S(2)}) async-start(), calls=%async_computation.10 | async-start | bytes 5242880 | tf_op jit(solution)/shard_map/all_gather | solution.py:45
  381.2 13.2 %all-to-all-start.1 = ((bf16[8,4,8192]{2,1,0:T(4,128)(2,1)}), bf16[8,4,8192]{2,1,0:T(4,128)(2,1)S(1)}, u32[]{:S(2)}, u32[]{:S(2)}) async-start(bf16[8,4,8192]{2,1,0:T(4,128)(2,1)} %copy.28), calls=%async_computation.3 | async-start | bytes 1048576 | tf_op jit(solution)/shard_map/all_to_all | solution.py:104
  384.7 102.8 %all-gather.15.cloned.1.call-start = ((), (), s32[]{:S(2)}) async-start(), calls=%async_computation.9 | async-start | bytes 1310720 | tf_op jit(solution)/shard_map/all_gather | solution.py:108
  395.7 74.0 %copy-start.2 = (bf16[16,8,1024]{2,1,0:T(8,128)(2,1)S(1)}, bf16[16,8,1024]{2,1,0:T(8,128)(2,1)}, u32[]{:S(2)}) copy-start(bf16[16,8,1024]{2,1,0:T(8,128)(2,1)} %param.13) | copy-start | bytes 786436
  395.7 147.6 %all-gather.19.cloned.1.call-start = ((), (), s32[]{:S(2)}) async-start(), calls=%async_computation.11 | async-start | bytes 9437184 | tf_op jit(solution)/shard_map/all_gather | solution.py:113
  471.3 13.4 %all-to-all-start = ((bf16[8,4,8192]{2,1,0:T(4,128)(2,1)}), bf16[8,4,8192]{2,1,0:T(4,128)(2,1)S(1)}, u32[]{:S(2)}, u32[]{:S(2)}) async-start(bf16[8,4,8192]{2,1,0:T(4,128)(2,1)} %copy.24), calls=%async_computation | async-start | bytes 1048576 | tf_op jit(solution)/shard_map/all_to_all | solution.py:103
Sparse Core Ops, SparseCore 0:
  8.9 83.4 all-gather.8
  94.3 54.4 all-gather.10
  152.3 71.2 reduce-scatter.2
  233.9 76.7 reduce-scatter.4
  313.5 54.8 all-gather.12
  378.6 80.7 all-gather.16
  461.0 26.4 all-gather.14
  489.4 53.8 all-gather.18
where the time goes:
time: 569 us
  waiting for transfers between devices  478 us (84%)
  matrix products  46.8 us (8%)
  between operations  13.7 us (2%)
  blocking collectives  11.8 us (2%)
  starting transfers between devices  7.87 us (1%)
  local copies, waits for them, and re-layouts  6.58 us (1%)
    all_gather x1, waiting for transfers between devices, body(): out_rows = lax.all_gather(basis_out, 'tensor', axis=1, tiled=True)  84.4 us
    reduce_scatter x1, waiting for transfers between devices, body(): lax.psum_scatter(jnp.einsum('kj,iqk->jqi', columns, rotated, preferred_el...  74.9 us
    reduce_scatter x1, waiting for transfers between devices, body(): lax.psum_scatter(jnp.einsum('ki,qkj->iqj', columns, queries, preferred_el...  74.8 us
    all_gather x1, waiting for transfers between devices, body(): lax.all_gather(turned, 'tensor', axis=0, tiled=True)  63.5 us
    all_gather x1, waiting for transfers between devices, body(): lax.all_gather(precond, 'example', axis=2, tiled=True)  55.8 us
    all_gather x1, waiting for transfers between devices, body(): lax.all_gather(scaled, 'example', axis=2, tiled=True)  54.8 us
    all_gather x1, waiting for transfers between devices, body(): in_rows = lax.all_gather(basis_in, 'example', axis=1, tiled=True)  47.3 us
    psum x1, blocking collectives, body(): lax.psum(partial_scores, 'tensor').reshape(query_total, list_len, token_len)  11.8 us
  transfers between devices with their start and end apart: 10, of which 10 were waited for; matrix products, arithmetic and copies ran while one was open for 5% of the time, Pallas kernels for 0%

commit v1 on v0

--- a/solution.py
+++ b/solution.py
@@ -1,7 +1,32 @@
+import functools
 import jax
 import jax.numpy as jnp
 from jax import lax
 from jax.sharding import PartitionSpec as P
+from jax.lax import axis_index, axis_size, ppermute
+
+
+def _deliver_threads(m, peer_axis):
+    mat_out, o_now, far_arr = (axis_size(peer_axis), axis_index(peer_axis), m.shape[2])
+    everything, val2 = (m, 1)
+    while val2 < mat_out:
+        everything = jnp.concatenate(
+            [
+                everything,
+                ppermute(
+                    everything,
+                    peer_axis,
+                    [(dev_j, (dev_j - val2) % mat_out) for dev_j in range(mat_out)],
+                ),
+            ],
+            axis=2,
+        )
+        val2 = 2 * val2
+    now = jnp.roll(everything, o_now * far_arr, axis=2)
+    return now
+
+
+terms_match = functools.partial(_deliver_threads, peer_axis="example")
 
 
 def body(
@@ -33,10 +58,7 @@
     scaled = (core_sum / eigvals[:, None, :]).astype(jnp.bfloat16)
     columns = out_rows
     turned = jnp.einsum(
-        "jqk,ik->jqi",
-        lax.all_gather(scaled, "example", axis=2, tiled=True),
-        columns,
-        preferred_element_type=jnp.float32,
+        "jqk,ik->jqi", terms_match(scaled), columns, preferred_element_type=jnp.float32
     ).astype(jnp.bfloat16)
     columns = in_rows
     precond = jnp.einsum(

time: 569 us -> 682 us (1.20)
  waiting for transfers between devices: 478 us -> 571 us
  local copies, waits for them, and re-layouts: 6.58 us -> 23.2 us
    ppermute x0 -> x3, waiting for transfers between devices: none -> 148 us  [_deliver_threads(): ppermute(everything, peer_axis, [(dev_j, (dev_j - val2) % mat_out) for de...]
    all_gather x1 -> x0, waiting for transfers between devices: 54.8 us -> none  [body(): lax.all_gather(scaled, 'example', axis=2, tiled=True)]
    unnamed x13 -> x27, local copies, waits for them, and re-layouts: 1.96 us -> 14.1 us
  transfers between devices with their start and end apart: 10 -> 12, of which waited for: 10 -> 12; matrix products, arithmetic and copies ran while one was open for 5% -> 5% of each run, Pallas kernels for 0% -> 0%
where the time goes in v1:
time: 682 us
  waiting for transfers between devices  571 us (84%)
  matrix products  45.1 us (7%)
  local copies, waits for them, and re-layouts  23.2 us (3%)
  between operations  13.7 us (2%)
  blocking collectives  11.8 us (2%)
  starting transfers between devices  10.8 us (2%)
    ppermute x3, waiting for transfers between devices, _deliver_threads(): ppermute(everything, peer_axis, [(dev_j, (dev_j - val2) % mat_out) for de...  148 us
    all_gather x1, waiting for transfers between devices, body(): out_rows = lax.all_gather(basis_out, 'tensor', axis=1, tiled=True)  84.4 us
    reduce_scatter x1, waiting for transfers between devices, body(): lax.psum_scatter(jnp.einsum('kj,iqk->jqi', columns, rotated, preferred_el...  74.9 us
    reduce_scatter x1, waiting for transfers between devices, body(): lax.psum_scatter(jnp.einsum('ki,qkj->iqj', columns, queries, preferred_el...  74.8 us
    all_gather x1, waiting for transfers between devices, body(): lax.all_gather(turned, 'tensor', axis=0, tiled=True)  62.7 us
    all_gather x1, waiting for transfers between devices, body(): lax.all_gather(precond, 'example', axis=2, tiled=True)  55.8 us
    all_gather x1, waiting for transfers between devices, body(): in_rows = lax.all_gather(basis_in, 'example', axis=1, tiled=True)  47.3 us
    unnamed x27, local copies, waits for them, and re-layouts  14.1 us
  transfers between devices with their start and end apart: 12, of which 12 were waited for; matrix products, arithmetic and copies ran while one was open for 5% of the time, Pallas kernels for 0%

profile of v1, /device:TPU:0, one launch (start us, length us, event | category | flops | bytes accessed | tf_op | source)
XLA Modules:
  0.0 681.6 jit_solution(3922233767656994828)
XLA Ops:
  6.5 0.7 all-gather.8.cloned.1.call-update
  7.3 0.0 all-gather.10.cloned.1.call-start
  7.3 0.7 all-gather.10.cloned.1.call-update
  8.0 0.0 reduce-scatter.3.cloned.1.call-start
  8.1 84.4 %all-gather.8.cloned.1.call-done = bf16[512,4096]{1,0:T(8,128)(2,1)} async-done(((bf16[512,1024]{1,0:T(8,128)(2,1)}), bf16[512,4096]{1,0:T(8,128)(2,1)}) %all-gather.8.cloned.1.call-update) | async-done | bytes 4194320 | tf_op jit(solution)/shard_map/all_gather | solution.py:37
  92.4 9.0 %convert_bitcast_fusion = bf16[4096,1,1024]{2,0,1:T(8,128)(2,1)} fusion(bf16[512,4096]{1,0:T(8,128)(2,1)} %all-gather.8.cloned.1.call-done, bf16[1,512,1024]{2,1,0:T(8,128)(2,1)S(1)} %copy-done), kind=kOutput, calls=%fused_computation.10 | convolution fusion | flops 4299161600 | bytes 13631488 | tf_op jit(solution)/shard_map/ki,qkj->iqj/dot_general | solution.py:42
  101.5 0.0 reduce-scatter.3.cloned.1.call-update
  101.5 0.0 reduce-scatter.5.cloned.1.call-start
  101.5 47.3 %all-gather.10.cloned.1.call-done = bf16[1024,4096]{1,0:T(8,128)(2,1)} async-done(((bf16[1024,512]{1,0:T(8,128)(2,1)}), bf16[1024,4096]{1,0:T(8,128)(2,1)}) %all-gather.10.cloned.1.call-update) | async-done | bytes 8388624 | tf_op jit(solution)/shard_map/all_gather | solution.py:38
  148.8 74.8 %reduce-scatter.3.cloned.1.call-done = bf16[512,1,1024]{2,0,1:T(8,128)(2,1)} async-done(((bf16[4096,1,1024]{2,0,1:T(8,128)(2,1)}), bf16[512,1,1024]{2,0,1:T(8,128)(2,1)}) %reduce-scatter.3.cloned.1.call-update) | async-done | bytes 1048592 | tf_op jit(solution)/shard_map/reduce_scatter | solution.py:41
  223.6 10.2 %fusion.6 = bf16[4096,1,512]{0,2,1:T(8,128)(2,1)} fusion(bf16[1024,4096]{1,0:T(8,128)(2,1)} %all-gather.10.cloned.1.call-done, bf16[512,1,1024]{2,0,1:T(8,128)(2,1)} %reduce-scatter.3.cloned.1.call-done), kind=kOutput, calls=%fused_computation.12 | convolution fusion | flops 4297064448 | bytes 13631488 | tf_op jit(solution)/shard_map/kj,iqk->jqi/dot_general | solution.py:51
  233.8 0.0 reduce-scatter.5.cloned.1.call-update
  233.8 0.0 all-gather.14.cloned.1.call-start
  233.9 1.9 copy.26
  235.8 74.9 %reduce-scatter.5.cloned.1.call-done = bf16[1024,1,512]{0,2,1:T(8,128)(2,1)} async-done(((bf16[4096,1,512]{0,2,1:T(8,128)(2,1)}), bf16[1024,1,512]{0,2,1:T(8,128)(2,1)}) %reduce-scatter.5.cloned.1.call-update) | async-done | bytes 1048592 | tf_op jit(solution)/shard_map/reduce_scatter | solution.py:50
  310.7 2.7 constant_dynamic-update-slice_fusion.7
  313.5 1.8 collective-permute-start
  315.3 12.3 %collective-permute-done = bf16[1024,1,512]{0,2,1:T(8,128)(2,1)S(1)} collective-permute-done((bf16[1024,1,512]{0,2,1:T(8,128)(2,1)S(1)}, bf16[1024,1,512]{0,2,1:T(8,128)(2,1)S(1)}, u32[]{:S(2)}, u32[]{:S(2)}) %collective-permute-start) | collective-permute-done | bytes 1048608 | tf_op jit(solution)/shard_map/ppermute | solution.py:16
  327.6 0.3 pad_maximum_fusion.1
  327.9 0.8 collective-permute-start.1
  328.7 47.5 %collective-permute-done.1 = bf16[1024,1,1024]{0,2,1:T(8,128)(2,1)S(1)} collective-permute-done((bf16[1024,1,1024]{0,2,1:T(8,128)(2,1)S(1)}, bf16[1024,1,1024]{0,2,1:T(8,128)(2,1)S(1)}, u32[]{:S(2)}, u32[]{:S(2)}) %collective-permute-start.1) | collective-permute-done | bytes 2097184 | tf_op jit(solution)/shard_map/ppermute | solution.py:16
  376.2 2.3 pad_maximum_fusion
  378.5 0.5 collective-permute-start.2
  379.1 2.4 constant_dynamic-update-slice_fusion.6
  381.5 1.5 constant_dynamic-update-slice_fusion.5
  382.9 88.2 %collective-permute-done.2 = bf16[1024,1,2048]{0,2,1:T(8,128)(2,1)} collective-permute-done((bf16[1024,1,2048]{0,2,1:T(8,128)(2,1)}, bf16[1024,1,2048]{0,2,1:T(8,128)(2,1)}, u32[]{:S(2)}, u32[]{:S(2)}) %collective-permute-start.2) | collective-permute-done | bytes 4194336 | tf_op jit(solution)/shard_map/ppermute | solution.py:16
  471.1 4.6 constant_dynamic-update-slice_fusion.4
  475.7 1.1 constant_dynamic-update-slice_fusion.3
  476.8 1.1 constant_dynamic-update-slice_fusion.2
  477.9 1.5 constant_dynamic-update-slice_fusion.1
  479.4 4.6 constant_dynamic-update-slice_fusion
  484.0 8.3 %fusion.8 = bf16[1024,512]{1,0:T(8,128)(2,1)} fusion(bf16[512,4096]{1,0:T(8,128)(2,1)S(1)} %copy-done.9, bf16[1024,1,8192]{0,2,1:T(8,128)(2,1)} %constant_dynamic-update-slice_fusion, s32[]{:T(128)S(6)} %select_n.62), kind=kOutput, calls=%fused_computation.17 | convolution fusion | flops 4295491584 | bytes 13631492 | tf_op jit(solution)/shard_map/jqk,ik->jqi/dot_general | solution.py:60
  492.3 0.0 all-gather.14.cloned.1.call-update
  492.3 0.1 reshape.275
  492.5 0.4 select_reduce_fusion.1
  492.9 0.3 convert_reduce_fusion.1
  493.3 0.1 iota_compare_fusion
  493.4 0.2 convert_reduce_fusion
  493.5 0.3 convolution_convert_fusion
  493.8 1.2 copy.28
  495.0 3.5 all-to-all-start.1
  498.5 0.0 all-gather.12.cloned.1.call-start
  498.6 9.6 %all-to-all-done.1 = bf16[8,4,8192]{2,1,0:T(4,128)(2,1)S(1)} async-done(((bf16[8,4,8192]{2,1,0:T(4,128)(2,1)}), bf16[8,4,8192]{2,1,0:T(4,128)(2,1)S(1)}, u32[]{:S(2)}, u32[]{:S(2)}) %all-to-all-start.1) | async-done | bytes 524320 | tf_op jit(solution)/shard_map/all_to_all | solution.py:126
  508.2 0.4 fusion.2
  508.6 0.8 reshape.265
  509.4 0.0 all-gather.12.cloned.1.call-update
  509.4 0.3 all-gather.16.cloned.1.call-start
  509.7 62.7 %all-gather.14.cloned.1.call-done = bf16[4096,512]{1,0:T(8,128)(2,1)} async-done(((bf16[1024,512]{1,0:T(8,128)(2,1)}), bf16[4096,512]{1,0:T(8,128)(2,1)}) %all-gather.14.cloned.1.call-update) | async-done | bytes 4194320 | tf_op jit(solution)/shard_map/all_gather | solution.py:67
  572.4 10.2 %fusion.11 = bf16[1024,512]{0,1:T(8,128)(2,1)} fusion(bf16[4096,512]{1,0:T(8,128)(2,1)} %all-gather.14.cloned.1.call-done, bf16[1024,4096]{1,0:T(8,128)(2,1)} %all-gather.10.cloned.1.call-done), kind=kOutput, calls=%fused_computation.19 | convolution fusion | flops 4295491584 | bytes 13631488 | tf_op jit(solution)/shard_map/jk,kqi->jqi/dot_general | solution.py:64
  582.6 0.1 reshape.273
  582.8 0.3 convolution_convert_fusion.1
  583.0 1.2 copy.24
  584.2 3.7 all-to-all-start
  587.9 9.7 %all-to-all-done = bf16[8,4,8192]{2,1,0:T(4,128)(2,1)S(1)} async-done(((bf16[8,4,8192]{2,1,0:T(4,128)(2,1)}), bf16[8,4,8192]{2,1,0:T(4,128)(2,1)S(1)}, u32[]{:S(2)}, u32[]{:S(2)}) %all-to-all-start) | async-done | bytes 524320 | tf_op jit(solution)/shard_map/all_to_all | solution.py:125
  597.7 0.4 fusion.1
  598.1 0.1 reshape.268
  598.2 0.2 copy.30
  598.4 1.9 all-gather.12.cloned.1.call-done
  600.3 55.8 %all-gather.16.cloned.1.call-done = bf16[1024,4096]{0,1:T(8,128)(2,1)} async-done(((bf16[1024,512]{0,1:T(8,128)(2,1)}), bf16[1024,4096]{0,1:T(8,128)(2,1)}) %all-gather.16.cloned.1.call-update) | async-done | bytes 8388624 | tf_op jit(solution)/shard_map/all_gather | solution.py:135
  656.1 6.0 fusion.13
  662.1 0.1 reshape.266
  662.2 11.8 %psum.7 = f32[1,16,8]{2,1,0:T(8,128)S(1)} all-reduce(f32[1,16,8]{2,1,0:T(8,128)S(1)} %reshape.266), channel_id=1, replica_groups=mesh['tensor'=4,'example'=8] {'tensor'}, use_global_device_ids=true, to_apply=%region_7.8 | all-reduce | flops 128 | bytes 1024 | tf_op jit(solution)/shard_map/psum | solution.py:139
  674.0 0.1 fusion.19
  674.1 0.7 copy.31
  (30 shorter events, 0.1 us)
Async XLA Ops:
  6.5 85.9 %copy-start = (bf16[1,512,1024]{2,1,0:T(8,128)(2,1)S(1)}, bf16[1,512,1024]{2,1,0:T(8,128)(2,1)}, u32[]{:S(2)}) copy-start(bf16[1,512,1024]{2,1,0:T(8,128)(2,1)} %param.9) | copy-start | bytes 3145732
  6.5 85.9 %all-gather.8.cloned.1.call-start = ((), (), s32[]{:S(2)}) async-start(), calls=%async_computation.4 | async-start | bytes 5242880 | tf_op jit(solution)/shard_map/all_gather | solution.py:37
  7.3 141.6 %all-gather.10.cloned.1.call-start = ((), (), s32[]{:S(2)}) async-start(), calls=%async_computation.6 | async-start | bytes 9437184 | tf_op jit(solution)/shard_map/all_gather | solution.py:38
  8.0 215.6 %reduce-scatter.3.cloned.1.call-start = ((), (), s32[]{:S(2)}) async-start(), calls=%async_computation.5 | async-start | bytes 9437184 | tf_op jit(solution)/shard_map/reduce_scatter | solution.py:41
  101.5 209.2 %reduce-scatter.5.cloned.1.call-start = ((), (), s32[]{:S(2)}) async-start(), calls=%async_computation.7 | async-start | bytes 5242880 | tf_op jit(solution)/shard_map/reduce_scatter | solution.py:50
  233.8 338.6 %all-gather.14.cloned.1.call-start = ((), (), s32[]{:S(2)}) async-start(), calls=%async_computation.9 | async-start | bytes 5242880 | tf_op jit(solution)/shard_map/all_gather | solution.py:67
  313.5 14.2 %collective-permute-start = (bf16[1024,1,512]{0,2,1:T(8,128)(2,1)S(1)}, bf16[1024,1,512]{0,2,1:T(8,128)(2,1)S(1)}, u32[]{:S(2)}, u32[]{:S(2)}) collective-permute-start(bf16[1024,1,512]{0,2,1:T(8,128)(2,1)S(1)} %get-tuple-element.8), channel_id=1, source_target_pairs={{0,7},{1,0},{2,1},{3,2},{4,3},{5,4},{6,5},{7,6},{8,15},{9,8},{10,9... | collective-permute-start | bytes 3145736 | tf_op jit(solution)/shard_map/ppermute | solution.py:16
  327.6 48.6 %copy-start.2 = (bf16[1024,1,512]{0,2,1:T(8,128)(2,1)}, bf16[1024,1,512]{0,2,1:T(8,128)(2,1)S(1)}, u32[]{:S(2)}) copy-start(bf16[1024,1,512]{0,2,1:T(8,128)(2,1)S(1)} %collective-permute-done) | copy-start | bytes 3145732
  327.9 48.3 %collective-permute-start.1 = (bf16[1024,1,1024]{0,2,1:T(8,128)(2,1)S(1)}, bf16[1024,1,1024]{0,2,1:T(8,128)(2,1)S(1)}, u32[]{:S(2)}, u32[]{:S(2)}) collective-permute-start(bf16[1024,1,1024]{0,2,1:T(8,128)(2,1)S(1)} %pad_maximum_fusion.1), channel_id=1, source_target_pairs={{0,6},{1,7},{2,0},{3,1},{4,2},{5,3},{6,4},{7,5},{8,14},{9,15},{10,... | collective-permute-start | bytes 6291464 | tf_op jit(solution)/shard_map/ppermute | solution.py:16
  378.5 92.6 %collective-permute-start.2 = (bf16[1024,1,2048]{0,2,1:T(8,128)(2,1)}, bf16[1024,1,2048]{0,2,1:T(8,128)(2,1)}, u32[]{:S(2)}, u32[]{:S(2)}) collective-permute-start(bf16[1024,1,2048]{0,2,1:T(8,128)(2,1)} %pad_maximum_fusion), channel_id=1, source_target_pairs={{0,4},{1,5},{2,6},{3,7},{4,0},{5,1},{6,2},{7,3},{8,12},{9,13},{10,... | collective-permute-start | bytes 12582920 | tf_op jit(solution)/shard_map/ppermute | solution.py:16
  379.1 97.8 %copy-start.3 = (bf16[1024,1,512]{0,2,1:T(8,128)(2,1)S(1)}, bf16[1024,1,512]{0,2,1:T(8,128)(2,1)}, u32[]{:S(2)}) copy-start(bf16[1024,1,512]{0,2,1:T(8,128)(2,1)} %copy-done.2) | copy-start | bytes 3145732
  475.7 8.2 %copy-start.9 = (bf16[512,4096]{1,0:T(8,128)(2,1)S(1)}, bf16[512,4096]{1,0:T(8,128)(2,1)}, u32[]{:S(2)}) copy-start(bf16[512,4096]{1,0:T(8,128)(2,1)} %all-gather.8.cloned.1.call-done) | copy-start | bytes 12582916
  483.9 8.4 %copy-start.4 = (bf16[16,8,1024]{2,1,0:T(8,128)(2,1)S(1)}, bf16[16,8,1024]{2,1,0:T(8,128)(2,1)}, u32[]{:S(2)}) copy-start(bf16[16,8,1024]{2,1,0:T(8,128)(2,1)} %param.14) | copy-start | bytes 786436
  484.0 8.5 %copy-start.6 = (s32[8,16]{1,0:T(8,128)S(1)}, s32[8,16]{1,0:T(8,128)}, u32[]{:S(2)}) copy-start(s32[8,16]{1,0:T(8,128)} %param.16) | copy-start | bytes 1540
  484.0 8.5 %copy-start.7 = (s32[128]{0:T(128)S(1)}, s32[128]{0:T(128)}, u32[]{:S(2)}) copy-start(s32[128]{0:T(128)} %param.17) | copy-start | bytes 1540
  484.0 8.5 %copy-start.8 = (s32[128]{0:T(128)S(1)}, s32[128]{0:T(128)}, u32[]{:S(2)}) copy-start(s32[128]{0:T(128)} %param.15) | copy-start | bytes 1540
  495.0 13.2 %all-to-all-start.1 = ((bf16[8,4,8192]{2,1,0:T(4,128)(2,1)}), bf16[8,4,8192]{2,1,0:T(4,128)(2,1)S(1)}, u32[]{:S(2)}, u32[]{:S(2)}) async-start(bf16[8,4,8192]{2,1,0:T(4,128)(2,1)} %copy.28), calls=%async_computation.3 | async-start | bytes 1048576 | tf_op jit(solution)/shard_map/all_to_all | solution.py:126
  498.5 101.8 %all-gather.12.cloned.1.call-start = ((), (), s32[]{:S(2)}) async-start(), calls=%async_computation.8 | async-start | bytes 1310720 | tf_op jit(solution)/shard_map/all_gather | solution.py:130
  509.4 73.2 %copy-start.5 = (bf16[16,8,1024]{2,1,0:T(8,128)(2,1)S(1)}, bf16[16,8,1024]{2,1,0:T(8,128)(2,1)}, u32[]{:S(2)}) copy-start(bf16[16,8,1024]{2,1,0:T(8,128)(2,1)} %param.13) | copy-start | bytes 786436
  509.4 146.7 %all-gather.16.cloned.1.call-start = ((), (), s32[]{:S(2)}) async-start(), calls=%async_computation.10 | async-start | bytes 9437184 | tf_op jit(solution)/shard_map/all_gather | solution.py:135
  582.6 92.2 %copy-start.1 = (bf16[1,512,1024]{2,1,0:T(8,128)(2,1)S(1)}, bf16[1,512,1024]{2,1,0:T(8,128)(2,1)}, u32[]{:S(2)}) copy-start(bf16[1,512,1024]{2,1,0:T(8,128)(2,1)} %param.9) | copy-start | bytes 3145732
  584.2 13.4 %all-to-all-start = ((bf16[8,4,8192]{2,1,0:T(4,128)(2,1)}), bf16[8,4,8192]{2,1,0:T(4,128)(2,1)S(1)}, u32[]{:S(2)}, u32[]{:S(2)}) async-start(bf16[8,4,8192]{2,1,0:T(4,128)(2,1)} %copy.24), calls=%async_computation | async-start | bytes 1048576 | tf_op jit(solution)/shard_map/all_to_all | solution.py:125
Sparse Core Ops, SparseCore 0:
  8.9 83.4 all-gather.7
  94.3 54.4 all-gather.9
  152.3 71.2 reduce-scatter.2
  233.9 76.7 reduce-scatter.4
  492.4 79.9 all-gather.13
  573.8 26.4 all-gather.11
  602.2 53.8 all-gather.15
